TPU v7x, 32 devices: a whole 2x2x4 slice. The times are simulated.
32 devices in a mesh: frame: 8 (over z, x), row: 4 (over y, core).
Axes of the slice: x: 2, y: 2, z: 4, core: 2. Of those that a mesh axis runs over, the one named last changes fastest.
Arguments:
- frames: float32 [64, 128, 2048], P('frame', 'row'), may hold values from -12 to 12
Outputs:
- estimate: float32 [128, 2048], P('row')
All inputs are finite; a program needn't handle non-finite values.
Results may differ from a plain program's by a relative error of at most 0.00002.
Values sent between devices are 32-bit elements; how exact they have to be, the bound alone decides.
No kernel may reach another device: no remote copies, remote signals or barrier semaphores. Data moves between devices by JAX's collectives and lax.ppermute only.
A program may use at most 64 MiB of HBM per device.

v0:
```python
import jax
import jax.numpy as jnp
from jax import lax
from jax.sharding import PartitionSpec as P

FRAMES = 64
ROUNDS = 3
GUIDE_EPS = 0.05
CAUCHY_SCALE = 0.5


def with_halo(x, sides, width):
    for axis, dim in sides:
        count, length = (lax.axis_size(axis), x.shape[dim])
        up = [(i, (i + 1) % count) for i in range(count - 1)]
        down = [(j, i) for i, j in up]
        last = lax.slice_in_dim(x, length - width, length, axis=dim)
        initial = lax.slice_in_dim(x, 0, width, axis=dim)
        before = lax.ppermute(last, axis, up)
        after = lax.ppermute(initial, axis, down)
        x = jnp.concatenate([before, x, after], axis=dim)
    return x


def row_sum(field):
    length = field.shape[-2] - 8
    total = field[..., 0:length, :]
    for offset in range(1, 9):
        total = total + field[..., offset : offset + length, :]
    return total


def col_sum(field):
    width = field.shape[-1]
    padded = jnp.pad(field, [(0, 0)] * (field.ndim - 1) + [(4, 4)])
    total = padded[..., 0:width]
    for offset in range(1, 9):
        total = total + padded[..., offset : offset + width]
    return total


def window_count(first, length, limit):
    place = first + jnp.arange(length, dtype=jnp.int32)
    lower = jnp.maximum(place - 4, 0)
    upper = jnp.minimum(place + 4, limit - 1)
    return jnp.maximum(upper - lower + 1, 1).astype(jnp.float32)


def smooth(padded_rows, area):
    return col_sum(row_sum(padded_rows)) / area


def shards(frames):
    local_rows = frames.shape[1]
    width = frames.shape[2]
    height = local_rows * lax.axis_size("row")
    start = lax.axis_index("row") * local_rows
    col_counts = window_count(0, width, width)
    estimate = lax.psum(jnp.sum(frames, axis=0), "frame") / FRAMES
    depth = 4
    padded_frames = with_halo(frames, (("row", 1),), 4)
    stat_rows = local_rows + 2 * depth - 8
    stat_first = start - depth + 4
    stat_area = window_count(stat_first, stat_rows, height)[:, None] * col_counts[None, :]
    out_area = window_count(start, local_rows, height)[:, None] * col_counts[None, :]
    for round_index in range(ROUNDS):
        padded_guide = with_halo(estimate, (("row", 0),), 4)
        mean_guide = smooth(padded_guide, stat_area)
        variance = smooth(padded_guide * padded_guide, stat_area) - mean_guide * mean_guide
        mean_frame = smooth(padded_frames, stat_area)
        cross = smooth(padded_guide[None] * padded_frames, stat_area)
        slope = (cross - mean_guide * mean_frame) / (variance + GUIDE_EPS)
        offset_term = mean_frame - slope * mean_guide
        stacked = with_halo(jnp.stack((slope, offset_term)), (("row", 2),), 4)
        slope_rows = stacked[0]
        offset_rows = stacked[1]
        filtered = smooth(slope_rows, out_area) * estimate[None] + smooth(offset_rows, out_area)
        gap = (filtered - estimate[None]) / CAUCHY_SCALE
        weight = 1.0 / (1.0 + gap * gap)
        weighted = jnp.sum(weight * frames, axis=0)
        total = jnp.sum(weight, axis=0)
        sums = lax.psum((weighted, total), "frame")
        estimate = sums[0] / sums[1]
    return estimate


def solution(mesh):
    return jax.shard_map(
        shards,
        mesh=mesh,
        in_specs=(P("frame", "row", None),),
        out_specs=P("row", None),
        check_vma=False,
    )
```

profile of v0, /device:TPU:0, one launch (start us, length us, event | category | flops | bytes accessed | tf_op | source)
XLA Modules:
  0.0 464.5 jit_solution(2341321879455873204)
XLA Ops:
  7.8 2.4 collective-permute-start.2
  11.7 1.8 constant_dynamic-update-slice_fusion.1
  13.5 2.4 collective-permute-done.3
  16.0 3.6 fusion.7
  19.7 75.9 %all-reduce.24.cloned.1.call-done = f32[32,2048]{1,0:T(8,128)} async-done(((f32[32,2048]{1,0:T(8,128)}), f32[32,2048]{1,0:T(8,128)}) %all-reduce.24.cloned.1.call-update) | async-done | bytes 262160 | tf_op jit(solution)/shard_map/psum | solution.py:59
  99.2 3.5 collective-permute-done.1
  103.2 2.5 slice_add_fusion.64
  106.1 1.9 fusion.74
  108.0 14.9 %subtract_bitcast_fusion.2 = (f32[1,8,32,2048]{3,2,1,0:T(8,128)S(1)}, f32[8,32,2048]{2,1,0:T(8,128)S(1)}, f32[8,32,2048]{2,1,0:T(8,128)}) fusion(f32[32,2048]{1,0:T(8,128)} %get-tuple-element.29, f32[32,2048]{1,0:T(8,128)S(1)} %get-tuple-element.28, f32[32,2048]{1,0:T(8,128)S(1)} %get-tuple-element.58, f32[8,32,2048]{2,1,0:T(8,128)} %slice_add_fusion.64, ...), kind=kLoop, calls=%fused_computation.150 | loop fusion | flops 12058624 | bytes 11272192 | tf_op jit(solution)/shard_map/stack | solution.py:74
  123.1 4.6 collective-permute-start.4
  127.7 1.6 collective-permute-start.5
  129.3 2.2 collective-permute-done.5
  132.9 1.5 slice_add_fusion.56
  134.5 1.5 slice_add_fusion.48
  136.1 9.7 %fusion.102 = (f32[32,2048]{1,0:T(8,128)}, f32[32,2048]{1,0:T(8,128)}) fusion(f32[8,32,2048]{2,1,0:T(8,128)S(1)} %copy-done, f32[8,32,2048]{2,1,0:T(8,128)S(1)} %slice_add_fusion.48, f32[32,2048]{1,0:T(8,128)S(1)} %broadcast_multiply_fusion.4, f32[32,2048]{1,0:T(8,128)S(1)} %get-tuple-element.58, f32[8,32,2048]{2,1,0:T(8,128)S(1)} %slice_add_fusion.56), kind=kLoop, calls=%fused_computation.343 | loop fusion | flops 14548992 | bytes 7340032 | tf_op jit(solution)/shard_map/reduce_sum | solution.py:81
  145.8 77.5 %all-reduce.30.cloned.1.call-done = (f32[32,2048]{1,0:T(8,128)}, f32[32,2048]{1,0:T(8,128)}) async-done(((f32[32,2048]{1,0:T(8,128)}, f32[32,2048]{1,0:T(8,128)}), (f32[32,2048]{1,0:T(8,128)}, f32[32,2048]{1,0:T(8,128)})) %all-reduce.30.cloned.1.call-update) | async-done | bytes 524304 | tf_op jit(solution)/shard_map/psum | solution.py:82
  225.8 1.8 collective-permute-start.7
  227.6 3.0 collective-permute-done.7
  231.3 1.5 slice_add_fusion.40
  234.3 4.5 subtract_bitcast_fusion.1
  239.0 4.6 collective-permute-start.8
  245.1 2.3 collective-permute-done.9
  252.3 9.7 %fusion.101 = (f32[32,2048]{1,0:T(8,128)}, f32[32,2048]{1,0:T(8,128)}) fusion(f32[8,32,2048]{2,1,0:T(8,128)S(1)} %copy-done, f32[8,32,2048]{2,1,0:T(8,128)S(1)} %slice_add_fusion.24, f32[32,2048]{1,0:T(8,128)S(1)} %div.158, f32[32,2048]{1,0:T(8,128)S(1)} %get-tuple-element.58, f32[8,32,2048]{2,1,0:T(8,128)S(1)} %slice_add_fusion.32), kind=kLoop, calls=%fused_computation.342 | loop fusion | flops 14548992 | bytes 7340032 | tf_op jit(solution)/shard_map/reduce_sum | solution.py:81
  262.1 77.6 %all-reduce.28.cloned.1.call-done = (f32[32,2048]{1,0:T(8,128)}, f32[32,2048]{1,0:T(8,128)}) async-done(((f32[32,2048]{1,0:T(8,128)}, f32[32,2048]{1,0:T(8,128)}), (f32[32,2048]{1,0:T(8,128)}, f32[32,2048]{1,0:T(8,128)})) %all-reduce.28.cloned.1.call-update) | async-done | bytes 524304 | tf_op jit(solution)/shard_map/psum | solution.py:82
  343.6 3.3 collective-permute-done.11
  350.6 4.5 subtract_bitcast_fusion
  355.3 4.6 collective-permute-start.12
  359.9 1.5 collective-permute-start.13
  361.5 2.2 collective-permute-done.13
  368.6 9.7 %fusion.100 = (f32[32,2048]{1,0:T(8,128)}, f32[32,2048]{1,0:T(8,128)}) fusion(f32[8,32,2048]{2,1,0:T(8,128)S(1)} %copy-done, f32[8,32,2048]{2,1,0:T(8,128)S(1)} %slice_add_fusion, f32[32,2048]{1,0:T(8,128)S(1)} %div.168, f32[32,2048]{1,0:T(8,128)S(1)} %get-tuple-element.58, f32[8,32,2048]{2,1,0:T(8,128)S(1)} %slice_add_fusion.8), kind=kLoop, calls=%fused_computation.341 | loop fusion | flops 14548992 | bytes 7340032 | tf_op jit(solution)/shard_map/reduce_sum | solution.py:81
  378.3 77.7 %all-reduce.26.cloned.1.call-done = (f32[32,2048]{1,0:T(8,128)}, f32[32,2048]{1,0:T(8,128)}) async-done(((f32[32,2048]{1,0:T(8,128)}, f32[32,2048]{1,0:T(8,128)}), (f32[32,2048]{1,0:T(8,128)}, f32[32,2048]{1,0:T(8,128)})) %all-reduce.26.cloned.1.call-update) | async-done | bytes 524304 | tf_op jit(solution)/shard_map/psum | solution.py:82
  456.0 1.8 div.178
  (67 shorter events, 32.8 us)
Async XLA Ops:
  6.5 89.1 %all-reduce.24.cloned.1.call-start = ((), (), s32[]{:S(2)}) async-start(), calls=%async_computation | async-start | bytes 524288 | tf_op jit(solution)/shard_map/psum | solution.py:59
  7.8 8.2 %collective-permute-start.2 = (f32[8,4,2048]{2,1,0:T(4,128)S(1)}, f32[8,4,2048]{2,1,0:T(4,128)S(1)}, u32[]{:S(2)}, u32[]{:S(2)}) collective-permute-start(f32[8,4,2048]{2,1,0:T(4,128)S(1)} %get-tuple-element.44), channel_id=1, source_target_pairs={{0,1},{1,2},{2,3},{4,5},{5,6},{6,7},{8,9},{9,10},{10,11},{12,13},{... | collective-permute-start | bytes 786440 | tf_op jit(solution)/shard_map/ppermute | solution.py:19
  10.3 5.8 %copy-start = (f32[8,32,2048]{2,1,0:T(8,128)S(1)}, f32[8,32,2048]{2,1,0:T(8,128)}, u32[]{:S(2)}) copy-start(f32[8,32,2048]{2,1,0:T(8,128)} %param.1) | copy-start | bytes 6291460
  10.3 5.7 %collective-permute-start.3 = (f32[8,4,2048]{2,1,0:T(4,128)S(1)}, f32[8,4,2048]{2,1,0:T(4,128)S(1)}, u32[]{:S(2)}, u32[]{:S(2)}) collective-permute-start(f32[8,4,2048]{2,1,0:T(4,128)S(1)} %get-tuple-element.45), channel_id=1, source_target_pairs={{1,0},{2,1},{3,2},{5,4},{6,5},{7,6},{9,8},{10,9},{11,10},{13,12},{... | collective-permute-start | bytes 786440 | tf_op jit(solution)/shard_map/ppermute | solution.py:20
  19.7 203.7 %all-reduce.30.cloned.1.call-start = ((), (), s32[]{:S(2)}) async-start(), calls=%async_computation.3 | async-start | bytes 1048576 | tf_op jit(solution)/shard_map/psum | solution.py:82
  96.6 2.6 collective-permute-start
  97.9 4.8 %collective-permute-start.1 = (f32[4,2048]{1,0:T(4,128)S(1)}, f32[4,2048]{1,0:T(4,128)S(1)}, u32[]{:S(2)}, u32[]{:S(2)}) collective-permute-start(f32[4,2048]{1,0:T(4,128)S(1)} %get-tuple-element.57), channel_id=1, source_target_pairs={{1,0},{2,1},{3,2},{5,4},{6,5},{7,6},{9,8},{10,9},{11,10},{13,12},{... | collective-permute-start | bytes 98312 | tf_op jit(solution)/shard_map/ppermute | solution.py:20
  105.7 2.3 copy-start.3
  123.1 6.2 %collective-permute-start.4 = (f32[2,8,4,2048]{3,2,1,0:T(4,128)S(1)}, f32[2,8,4,2048]{3,2,1,0:T(4,128)S(1)}, u32[]{:S(2)}, u32[]{:S(2)}) collective-permute-start(f32[2,8,4,2048]{3,2,1,0:T(4,128)S(1)} %get-tuple-element.40), channel_id=1, source_target_pairs={{0,1},{1,2},{2,3},{4,5},{5,6},{6,7},{8,9},{9,10},{10,11},{12,13},{... | collective-permute-start | bytes 1572872 | tf_op jit(solution)/shard_map/ppermute | solution.py:19
  127.7 3.8 collective-permute-start.5
  145.8 193.9 %all-reduce.28.cloned.1.call-start = ((), (), s32[]{:S(2)}) async-start(), calls=%async_computation.2 | async-start | bytes 1048576 | tf_op jit(solution)/shard_map/psum | solution.py:82
  224.5 3.1 collective-permute-start.6
  225.8 4.8 %collective-permute-start.7 = (f32[4,2048]{1,0:T(4,128)S(1)}, f32[4,2048]{1,0:T(4,128)S(1)}, u32[]{:S(2)}, u32[]{:S(2)}) collective-permute-start(f32[4,2048]{1,0:T(4,128)S(1)} %get-tuple-element.55), channel_id=1, source_target_pairs={{1,0},{2,1},{3,2},{5,4},{6,5},{7,6},{9,8},{10,9},{11,10},{13,12},{... | collective-permute-start | bytes 98312 | tf_op jit(solution)/shard_map/ppermute | solution.py:20
  231.3 3.0 copy-start.1
  239.0 6.1 %collective-permute-start.8 = (f32[2,8,4,2048]{3,2,1,0:T(4,128)S(1)}, f32[2,8,4,2048]{3,2,1,0:T(4,128)S(1)}, u32[]{:S(2)}, u32[]{:S(2)}) collective-permute-start(f32[2,8,4,2048]{3,2,1,0:T(4,128)S(1)} %get-tuple-element.38), channel_id=1, source_target_pairs={{0,1},{1,2},{2,3},{4,5},{5,6},{6,7},{8,9},{9,10},{10,11},{12,13},{... | collective-permute-start | bytes 1572872 | tf_op jit(solution)/shard_map/ppermute | solution.py:19
  243.6 3.8 collective-permute-start.9
  262.0 193.9 %all-reduce.26.cloned.1.call-start = ((), (), s32[]{:S(2)}) async-start(), calls=%async_computation.1 | async-start | bytes 1048576 | tf_op jit(solution)/shard_map/psum | solution.py:82
  340.8 2.8 collective-permute-start.10
  342.1 4.8 %collective-permute-start.11 = (f32[4,2048]{1,0:T(4,128)S(1)}, f32[4,2048]{1,0:T(4,128)S(1)}, u32[]{:S(2)}, u32[]{:S(2)}) collective-permute-start(f32[4,2048]{1,0:T(4,128)S(1)} %get-tuple-element.53), channel_id=1, source_target_pairs={{1,0},{2,1},{3,2},{5,4},{6,5},{7,6},{9,8},{10,9},{11,10},{13,12},{... | collective-permute-start | bytes 98312 | tf_op jit(solution)/shard_map/ppermute | solution.py:20
  347.6 3.0 copy-start.2
  355.3 6.1 %collective-permute-start.12 = (f32[2,8,4,2048]{3,2,1,0:T(4,128)S(1)}, f32[2,8,4,2048]{3,2,1,0:T(4,128)S(1)}, u32[]{:S(2)}, u32[]{:S(2)}) collective-permute-start(f32[2,8,4,2048]{3,2,1,0:T(4,128)S(1)} %get-tuple-element.36), channel_id=1, source_target_pairs={{0,1},{1,2},{2,3},{4,5},{5,6},{6,7},{8,9},{9,10},{10,11},{12,13},{... | collective-permute-start | bytes 1572872 | tf_op jit(solution)/shard_map/ppermute | solution.py:19
  359.9 3.8 collective-permute-start.13
Sparse Core Ops, SparseCore 0:
  19.8 75.7 all-reduce.23
  145.9 77.4 all-reduce.29
  262.2 77.4 all-reduce.27
  378.4 77.4 all-reduce.25
where the time goes:
time: 472 us; the launch traced here: 465 us
  waiting for transfers between devices  328 us (69%)
  other arithmetic  87.1 us (18%)
  starting transfers between devices  30.7 us (7%)
  between operations  13.9 us (3%)
  local copies, waits for them, and re-layouts  5.12 us (1%)
    psum x3, waiting for transfers between devices, shards(): sums = lax.psum((weighted, total), 'frame')  233 us
    psum x1, waiting for transfers between devices, shards(): estimate = lax.psum(jnp.sum(frames, axis=0), 'frame') / FRAMES  75.9 us
    reduce_sum x3, other arithmetic, shards(): total = jnp.sum(weight, axis=0)  29.1 us
    another operation x3, other arithmetic, shards(): stacked = with_halo(jnp.stack((slope, offset_term)), (('row', 2),), 4)  23.9 us
    ppermute x7, starting transfers between devices, with_halo(): before = lax.ppermute(last, axis, up)  20 us
    add x15, other arithmetic, row_sum(): total = total + field[..., offset:offset + length, :]  19.8 us
    ppermute x7, waiting for transfers between devices, with_halo(): after = lax.ppermute(initial, axis, down)  18.9 us
    ppermute x7, starting transfers between devices, with_halo(): after = lax.ppermute(initial, axis, down)  10.6 us
  transfers between devices with their start and end apart: 18, of which 11 were waited for; matrix products, arithmetic and copies ran while one was open for 0% of the time, Pallas kernels for 0%

commit v1 on v0

--- a/solution.py
+++ b/solution.py
@@ -1,3 +1,4 @@
+import functools
 import jax
 import jax.numpy as jnp
 from jax import lax
@@ -7,6 +8,14 @@
 ROUNDS = 3
 GUIDE_EPS = 0.05
 CAUCHY_SCALE = 0.5
+
+
+def _raise_ticks(frame, ax_name):
+    then = lax.all_gather(frame, ax_name).sum(axis=0)
+    return then
+
+
+remake_patch_now = functools.partial(_raise_ticks, ax_name="frame")
 
 
 def with_halo(x, sides, width):
@@ -56,7 +65,7 @@
     height = local_rows * lax.axis_size("row")
     start = lax.axis_index("row") * local_rows
     col_counts = window_count(0, width, width)
-    estimate = lax.psum(jnp.sum(frames, axis=0), "frame") / FRAMES
+    estimate = remake_patch_now(jnp.sum(frames, axis=0)) / FRAMES
     depth = 4
     padded_frames = with_halo(frames, (("row", 1),), 4)
     stat_rows = local_rows + 2 * depth - 8

time: 472 us -> 450 us (0.953)
  waiting for transfers between devices: 328 us -> 305 us
    psum x1 -> x0, waiting for transfers between devices: 75.9 us -> none  [shards(): estimate = lax.psum(jnp.sum(frames, axis=0), 'frame') / FRAMES]
    all_gather x0 -> x1, waiting for transfers between devices: none -> 53.9 us  [_raise_ticks(): then = lax.all_gather(frame, ax_name).sum(axis=0)]
where the time goes in v1:
time: 450 us; the launch traced here: 442 us
  waiting for transfers between devices  305 us (68%)
  other arithmetic  88 us (20%)
  starting transfers between devices  30.7 us (7%)
  between operations  13.9 us (3%)
  local copies, waits for them, and re-layouts  4.64 us (1%)
    psum x3, waiting for transfers between devices, shards(): sums = lax.psum((weighted, total), 'frame')  232 us
    all_gather x1, waiting for transfers between devices, _raise_ticks(): then = lax.all_gather(frame, ax_name).sum(axis=0)  53.9 us
    reduce_sum x3, other arithmetic, shards(): total = jnp.sum(weight, axis=0)  29.1 us
    another operation x3, other arithmetic, shards(): stacked = with_halo(jnp.stack((slope, offset_term)), (('row', 2),), 4)  23.9 us
    ppermute x7, starting transfers between devices, with_halo(): before = lax.ppermute(last, axis, up)  20 us
    add x15, other arithmetic, row_sum(): total = total + field[..., offset:offset + length, :]  19.8 us
    ppermute x7, waiting for transfers between devices, with_halo(): after = lax.ppermute(initial, axis, down)  18.9 us
    ppermute x7, starting transfers between devices, with_halo(): after = lax.ppermute(initial, axis, down)  10.6 us
  transfers between devices with their start and end apart: 18, of which 11 were waited for; matrix products, arithmetic and copies ran while one was open for 0% of the time, Pallas kernels for 0%

profile of v1, /device:TPU:0, one launch (start us, length us, event | category | flops | bytes accessed | tf_op | source)
XLA Modules:
  0.0 442.3 jit_solution(17504944280405846789)
XLA Ops:
  7.8 2.4 collective-permute-start.2
  11.7 1.8 constant_dynamic-update-slice_fusion.1
  13.5 2.4 collective-permute-done.3
  16.0 3.6 fusion.7
  19.7 53.9 %all-gather.3.cloned.1.call-done = f32[256,2048]{1,0:T(8,128)} async-done(((f32[32,2048]{1,0:T(8,128)}), f32[256,2048]{1,0:T(8,128)}) %all-gather.3.cloned.1.call-update) | async-done | bytes 2097168 | tf_op jit(solution)/shard_map/all_gather | solution.py:14
  73.6 1.7 reduce_sum.73
  78.0 3.5 collective-permute-done.1
  82.0 2.5 slice_add_fusion.64
  84.9 1.9 fusion.74
  86.8 14.9 %subtract_bitcast_fusion.2 = (f32[1,8,32,2048]{3,2,1,0:T(8,128)S(1)}, f32[8,32,2048]{2,1,0:T(8,128)S(1)}, f32[8,32,2048]{2,1,0:T(8,128)}) fusion(f32[32,2048]{1,0:T(8,128)} %get-tuple-element.29, f32[32,2048]{1,0:T(8,128)S(1)} %get-tuple-element.28, f32[32,2048]{1,0:T(8,128)S(1)} %get-tuple-element.58, f32[8,32,2048]{2,1,0:T(8,128)} %slice_add_fusion.64, ...), kind=kLoop, calls=%fused_computation.150 | loop fusion | flops 12058624 | bytes 11272192 | tf_op jit(solution)/shard_map/stack | solution.py:83
  101.9 4.6 %collective-permute-start.4 = (f32[2,8,4,2048]{3,2,1,0:T(4,128)S(1)}, f32[2,8,4,2048]{3,2,1,0:T(4,128)S(1)}, u32[]{:S(2)}, u32[]{:S(2)}) collective-permute-start(f32[2,8,4,2048]{3,2,1,0:T(4,128)S(1)} %get-tuple-element.40), channel_id=1, source_target_pairs={{0,1},{1,2},{2,3},{4,5},{5,6},{6,7},{8,9},{9,10},{10,11},{12,13},{... | collective-permute-start | bytes 1572872 | tf_op jit(solution)/shard_map/ppermute | solution.py:28
  106.5 1.6 collective-permute-start.5
  108.1 2.2 collective-permute-done.5
  111.6 1.5 slice_add_fusion.56
  113.1 1.5 slice_add_fusion.48
  114.7 9.7 %fusion.102 = (f32[32,2048]{1,0:T(8,128)}, f32[32,2048]{1,0:T(8,128)}) fusion(f32[8,32,2048]{2,1,0:T(8,128)S(1)} %copy-done, f32[8,32,2048]{2,1,0:T(8,128)S(1)} %slice_add_fusion.48, f32[32,2048]{1,0:T(8,128)S(1)} %broadcast_multiply_fusion.4, f32[32,2048]{1,0:T(8,128)S(1)} %get-tuple-element.58, f32[8,32,2048]{2,1,0:T(8,128)S(1)} %slice_add_fusion.56), kind=kLoop, calls=%fused_computation.343 | loop fusion | flops 14548992 | bytes 7340032 | tf_op jit(solution)/shard_map/reduce_sum | solution.py:90
  124.4 76.9 %all-reduce.27.cloned.1.call-done = (f32[32,2048]{1,0:T(8,128)}, f32[32,2048]{1,0:T(8,128)}) async-done(((f32[32,2048]{1,0:T(8,128)}, f32[32,2048]{1,0:T(8,128)}), (f32[32,2048]{1,0:T(8,128)}, f32[32,2048]{1,0:T(8,128)})) %all-reduce.27.cloned.1.call-update) | async-done | bytes 524304 | tf_op jit(solution)/shard_map/psum | solution.py:91
  203.7 1.8 collective-permute-start.7
  205.6 3.0 collective-permute-done.7
  212.2 4.5 %subtract_bitcast_fusion.1 = (f32[1,8,32,2048]{3,2,1,0:T(8,128)S(1)}, f32[8,32,2048]{2,1,0:T(8,128)S(1)}) fusion(f32[8,32,2048]{2,1,0:T(8,128)S(1)} %copy-done.1, f32[32,2048]{1,0:T(8,128)S(1)} %get-tuple-element.24, f32[32,2048]{1,0:T(8,128)S(1)} %get-tuple-element.23, f32[32,2048]{1,0:T(8,128)S(1)} %get-tuple-element.58, ...), kind=kLoop, calls=%fused_computation.131 | loop fusion | flops 7340032 | bytes 9175040 | tf_op jit(solution)/shard_map/stack | solution.py:83
  217.0 4.6 %collective-permute-start.8 = (f32[2,8,4,2048]{3,2,1,0:T(4,128)S(1)}, f32[2,8,4,2048]{3,2,1,0:T(4,128)S(1)}, u32[]{:S(2)}, u32[]{:S(2)}) collective-permute-start(f32[2,8,4,2048]{3,2,1,0:T(4,128)S(1)} %get-tuple-element.38), channel_id=1, source_target_pairs={{0,1},{1,2},{2,3},{4,5},{5,6},{6,7},{8,9},{9,10},{10,11},{12,13},{... | collective-permute-start | bytes 1572872 | tf_op jit(solution)/shard_map/ppermute | solution.py:28
  223.1 2.3 collective-permute-done.9
  230.1 9.7 %fusion.101 = (f32[32,2048]{1,0:T(8,128)}, f32[32,2048]{1,0:T(8,128)}) fusion(f32[8,32,2048]{2,1,0:T(8,128)S(1)} %copy-done, f32[8,32,2048]{2,1,0:T(8,128)S(1)} %slice_add_fusion.24, f32[32,2048]{1,0:T(8,128)S(1)} %div.158, f32[32,2048]{1,0:T(8,128)S(1)} %get-tuple-element.58, f32[8,32,2048]{2,1,0:T(8,128)S(1)} %slice_add_fusion.32), kind=kLoop, calls=%fused_computation.342 | loop fusion | flops 14548992 | bytes 7340032 | tf_op jit(solution)/shard_map/reduce_sum | solution.py:90
  239.9 77.6 %all-reduce.25.cloned.1.call-done = (f32[32,2048]{1,0:T(8,128)}, f32[32,2048]{1,0:T(8,128)}) async-done(((f32[32,2048]{1,0:T(8,128)}, f32[32,2048]{1,0:T(8,128)}), (f32[32,2048]{1,0:T(8,128)}, f32[32,2048]{1,0:T(8,128)})) %all-reduce.25.cloned.1.call-update) | async-done | bytes 524304 | tf_op jit(solution)/shard_map/psum | solution.py:91
  321.4 3.3 collective-permute-done.11
  328.4 4.5 %subtract_bitcast_fusion = (f32[1,8,32,2048]{3,2,1,0:T(8,128)S(1)}, f32[8,32,2048]{2,1,0:T(8,128)S(1)}) fusion(f32[8,32,2048]{2,1,0:T(8,128)S(1)} %copy-done.2, f32[32,2048]{1,0:T(8,128)S(1)} %get-tuple-element.20, f32[32,2048]{1,0:T(8,128)S(1)} %get-tuple-element.19, f32[32,2048]{1,0:T(8,128)S(1)} %get-tuple-element.58, f32[8,32,2048]{2,1,0:T(8,128)S(1)} %slice_add_fusion.16), kind=kLoop, calls=%fused_computation.112 | loop fusion | flops 7340032 | bytes 9175040 | tf_op jit(solution)/shard_map/stack | solution.py:83
  333.2 4.6 %collective-permute-start.12 = (f32[2,8,4,2048]{3,2,1,0:T(4,128)S(1)}, f32[2,8,4,2048]{3,2,1,0:T(4,128)S(1)}, u32[]{:S(2)}, u32[]{:S(2)}) collective-permute-start(f32[2,8,4,2048]{3,2,1,0:T(4,128)S(1)} %get-tuple-element.36), channel_id=1, source_target_pairs={{0,1},{1,2},{2,3},{4,5},{5,6},{6,7},{8,9},{9,10},{10,11},{12,13},{... | collective-permute-start | bytes 1572872 | tf_op jit(solution)/shard_map/ppermute | solution.py:28
  337.8 1.5 collective-permute-start.13
  339.4 2.2 collective-permute-done.13
  346.3 9.7 %fusion.100 = (f32[32,2048]{1,0:T(8,128)}, f32[32,2048]{1,0:T(8,128)}) fusion(f32[8,32,2048]{2,1,0:T(8,128)S(1)} %copy-done, f32[8,32,2048]{2,1,0:T(8,128)S(1)} %slice_add_fusion, f32[32,2048]{1,0:T(8,128)S(1)} %div.168, f32[32,2048]{1,0:T(8,128)S(1)} %get-tuple-element.58, f32[8,32,2048]{2,1,0:T(8,128)S(1)} %slice_add_fusion.8), kind=kLoop, calls=%fused_computation.341 | loop fusion | flops 14548992 | bytes 7340032 | tf_op jit(solution)/shard_map/reduce_sum | solution.py:90
  356.0 77.7 %all-reduce.23.cloned.1.call-done = (f32[32,2048]{1,0:T(8,128)}, f32[32,2048]{1,0:T(8,128)}) async-done(((f32[32,2048]{1,0:T(8,128)}, f32[32,2048]{1,0:T(8,128)}), (f32[32,2048]{1,0:T(8,128)}, f32[32,2048]{1,0:T(8,128)})) %all-reduce.23.cloned.1.call-update) | async-done | bytes 524304 | tf_op jit(solution)/shard_map/psum | solution.py:91
  433.7 1.8 div.178
  (68 shorter events, 33.0 us)
Async XLA Ops:
  6.5 67.1 %all-gather.3.cloned.1.call-start = ((), (), s32[]{:S(2)}) async-start(), calls=%async_computation | async-start | bytes 2359296 | tf_op jit(solution)/shard_map/all_gather | solution.py:14
  7.8 8.2 %collective-permute-start.2 = (f32[8,4,2048]{2,1,0:T(4,128)S(1)}, f32[8,4,2048]{2,1,0:T(4,128)S(1)}, u32[]{:S(2)}, u32[]{:S(2)}) collective-permute-start(f32[8,4,2048]{2,1,0:T(4,128)S(1)} %get-tuple-element.44), channel_id=1, source_target_pairs={{0,1},{1,2},{2,3},{4,5},{5,6},{6,7},{8,9},{9,10},{10,11},{12,13},{... | collective-permute-start | bytes 786440 | tf_op jit(solution)/shard_map/ppermute | solution.py:28
  10.3 5.8 %copy-start = (f32[8,32,2048]{2,1,0:T(8,128)S(1)}, f32[8,32,2048]{2,1,0:T(8,128)}, u32[]{:S(2)}) copy-start(f32[8,32,2048]{2,1,0:T(8,128)} %param.1) | copy-start | bytes 6291460
  10.3 5.7 %collective-permute-start.3 = (f32[8,4,2048]{2,1,0:T(4,128)S(1)}, f32[8,4,2048]{2,1,0:T(4,128)S(1)}, u32[]{:S(2)}, u32[]{:S(2)}) collective-permute-start(f32[8,4,2048]{2,1,0:T(4,128)S(1)} %get-tuple-element.45), channel_id=1, source_target_pairs={{1,0},{2,1},{3,2},{5,4},{6,5},{7,6},{9,8},{10,9},{11,10},{13,12},{... | collective-permute-start | bytes 786440 | tf_op jit(solution)/shard_map/ppermute | solution.py:29
  19.7 181.6 %all-reduce.27.cloned.1.call-start = ((), (), s32[]{:S(2)}) async-start(), calls=%async_computation.3 | async-start | bytes 1048576 | tf_op jit(solution)/shard_map/psum | solution.py:91
  75.4 2.6 collective-permute-start
  76.7 4.8 %collective-permute-start.1 = (f32[4,2048]{1,0:T(4,128)S(1)}, f32[4,2048]{1,0:T(4,128)S(1)}, u32[]{:S(2)}, u32[]{:S(2)}) collective-permute-start(f32[4,2048]{1,0:T(4,128)S(1)} %get-tuple-element.57), channel_id=1, source_target_pairs={{1,0},{2,1},{3,2},{5,4},{6,5},{7,6},{9,8},{10,9},{11,10},{13,12},{... | collective-permute-start | bytes 98312 | tf_op jit(solution)/shard_map/ppermute | solution.py:29
  84.5 2.3 copy-start.3
  101.9 6.2 %collective-permute-start.4 = (f32[2,8,4,2048]{3,2,1,0:T(4,128)S(1)}, f32[2,8,4,2048]{3,2,1,0:T(4,128)S(1)}, u32[]{:S(2)}, u32[]{:S(2)}) collective-permute-start(f32[2,8,4,2048]{3,2,1,0:T(4,128)S(1)} %get-tuple-element.40), channel_id=1, source_target_pairs={{0,1},{1,2},{2,3},{4,5},{5,6},{6,7},{8,9},{9,10},{10,11},{12,13},{... | collective-permute-start | bytes 1572872 | tf_op jit(solution)/shard_map/ppermute | solution.py:28
  106.5 3.8 collective-permute-start.5
  124.4 193.1 %all-reduce.25.cloned.1.call-start = ((), (), s32[]{:S(2)}) async-start(), calls=%async_computation.2 | async-start | bytes 1048576 | tf_op jit(solution)/shard_map/psum | solution.py:91
  202.4 3.1 collective-permute-start.6
  203.7 4.8 %collective-permute-start.7 = (f32[4,2048]{1,0:T(4,128)S(1)}, f32[4,2048]{1,0:T(4,128)S(1)}, u32[]{:S(2)}, u32[]{:S(2)}) collective-permute-start(f32[4,2048]{1,0:T(4,128)S(1)} %get-tuple-element.55), channel_id=1, source_target_pairs={{1,0},{2,1},{3,2},{5,4},{6,5},{7,6},{9,8},{10,9},{11,10},{13,12},{... | collective-permute-start | bytes 98312 | tf_op jit(solution)/shard_map/ppermute | solution.py:29
  209.2 3.0 copy-start.1
  217.0 6.1 %collective-permute-start.8 = (f32[2,8,4,2048]{3,2,1,0:T(4,128)S(1)}, f32[2,8,4,2048]{3,2,1,0:T(4,128)S(1)}, u32[]{:S(2)}, u32[]{:S(2)}) collective-permute-start(f32[2,8,4,2048]{3,2,1,0:T(4,128)S(1)} %get-tuple-element.38), channel_id=1, source_target_pairs={{0,1},{1,2},{2,3},{4,5},{5,6},{6,7},{8,9},{9,10},{10,11},{12,13},{... | collective-permute-start | bytes 1572872 | tf_op jit(solution)/shard_map/ppermute | solution.py:28
  221.6 3.8 collective-permute-start.9
  239.9 193.8 %all-reduce.23.cloned.1.call-start = ((), (), s32[]{:S(2)}) async-start(), calls=%async_computation.1 | async-start | bytes 1048576 | tf_op jit(solution)/shard_map/psum | solution.py:91
  318.6 2.8 collective-permute-start.10
  319.9 4.8 %collective-permute-start.11 = (f32[4,2048]{1,0:T(4,128)S(1)}, f32[4,2048]{1,0:T(4,128)S(1)}, u32[]{:S(2)}, u32[]{:S(2)}) collective-permute-start(f32[4,2048]{1,0:T(4,128)S(1)} %get-tuple-element.53), channel_id=1, source_target_pairs={{1,0},{2,1},{3,2},{5,4},{6,5},{7,6},{9,8},{10,9},{11,10},{13,12},{... | collective-permute-start | bytes 98312 | tf_op jit(solution)/shard_map/ppermute | solution.py:29
  325.4 3.0 copy-start.2
  333.2 6.1 %collective-permute-start.12 = (f32[2,8,4,2048]{3,2,1,0:T(4,128)S(1)}, f32[2,8,4,2048]{3,2,1,0:T(4,128)S(1)}, u32[]{:S(2)}, u32[]{:S(2)}) collective-permute-start(f32[2,8,4,2048]{3,2,1,0:T(4,128)S(1)} %get-tuple-element.36), channel_id=1, source_target_pairs={{0,1},{1,2},{2,3},{4,5},{5,6},{6,7},{8,9},{9,10},{10,11},{12,13},{... | collective-permute-start | bytes 1572872 | tf_op jit(solution)/shard_map/ppermute | solution.py:28
  337.8 3.8 collective-permute-start.13
Sparse Core Ops, SparseCore 0:
  19.8 53.7 all-gather.2
  124.5 76.7 all-reduce.26
  240.0 77.4 all-reduce.24
  356.2 77.4 all-reduce.22
